TPU v7x, 128 devices: a whole 4x4x4 slice. The times are simulated.
128 devices in a mesh: ctx: 32 (over z, x, y_lo), tp: 4 (over y_hi, core).
Axes of the slice: x: 4, y: 4 (y_hi: 2, y_lo: 2; y = y_hi * 2 + y_lo), z: 4, core: 2. Of those that a mesh axis runs over, the one named last changes fastest.
Arguments:
- signal: bfloat16 [4096, 2048], P('ctx', 'tp'), may hold values from -6 to 6
- gate: bfloat16 [4096, 2048], P('ctx', 'tp'), may hold values from -6 to 6
- filt: bfloat16 [4096, 2048], P('ctx', 'tp'), may hold values from -0.25 to 0.25
- bias: float32 [2048], P('tp'), may hold values from -2 to 2
- doc_ids: int32 [4096], replicated, may hold values from 0 to 3, never falling along the last dimension, each value on 1 to 3840 neighbouring positions
- block_perm: int32 [64], replicated, may hold values from 0 to 63, each once
- out_weight: bfloat16 [2048, 2048], P('tp'), may hold values from -0.125 to 0.125
Outputs:
- mixed: bfloat16 [4096, 2048], P('ctx', 'tp')
Inputs may be any that keep to these rules, and one draw needn't show every extreme that they name: `doc_ids`: ids never fall along the sequence; each document is a run of 1 to 3840 positions, one exactly 3840. `block_perm`: each block number once.
All inputs are finite; a program needn't handle non-finite values.
Results may differ from a plain program's by a relative error of at most 0.012.
Values may be sent and summed in bfloat16 or wider, within the bound.
No kernel may reach another device: no remote copies, remote signals or barrier semaphores. Data moves between devices by JAX's collectives and lax.ppermute only.
A program may use at most 64 MiB of HBM per device.

v0:
```python
import jax
import jax.numpy as jnp
from jax import lax
from jax.sharding import PartitionSpec as P

SPAN = 64
DOC_COUNT = 4


def skew_blocks(a, fill):
    chans, blocks, span = a.shape
    a_ext = jnp.concatenate([a, jnp.full_like(a, fill)], axis=1)
    tiled = jnp.broadcast_to(a_ext[:, None], (chans, blocks, 2 * blocks, span))
    tiled = tiled.reshape(chans, blocks * 2 * blocks, span)[:, : blocks * (2 * blocks - 1)]
    return tiled.reshape(chans, blocks, 2 * blocks - 1, span)[:, :, :blocks]


def block_conv(x_cm, f_cm, doc_ids):
    chans, seq = x_cm.shape
    span = SPAN
    blocks = seq // span
    width = seq + span
    f_ext = jnp.pad(f_cm, ((0, 0), (0, span)))
    tt = jnp.broadcast_to(f_ext[:, None, :], (chans, span, width)).reshape(chans, span * width)
    tt = tt[:, : span * (width - 1)].reshape(chans, span, width - 1)[:, :, :seq]
    tt = tt.reshape(chans, span, blocks, span)
    xb = x_cm.reshape(chans, blocks, span)
    src = skew_blocks(xb, 0)
    docb = doc_ids.reshape(blocks, span)
    lead = docb[:, 0]
    src_doc = skew_blocks(docb[None], -1)[0]
    keep = src_doc == lead[None, :, None]
    src = jnp.where(keep[None], src, jnp.zeros_like(src))
    lead_part = jnp.einsum("cjdi,cdtj->cit", tt, src, preferred_element_type=jnp.float32)
    row_doc = docb.T
    lead_rows = row_doc == lead[None, :]
    out = jnp.where(lead_rows[None], lead_part, 0.0)
    near = tt[:, :, 0, :]
    xt = jnp.swapaxes(xb, 1, 2)
    for doc in range(DOC_COUNT):
        member = docb.T == doc
        part = jnp.einsum(
            "cji,cjt->cit",
            near,
            jnp.where(member[None], xt, jnp.zeros_like(xt)),
            preferred_element_type=jnp.float32,
        )
        rows = member & (lead[None, :] != doc)
        out = out + jnp.where(rows[None], part, 0.0)
    return jnp.swapaxes(out, 1, 2).reshape(chans, seq)


def body(signal, gate, filt, bias, doc_ids, block_perm, out_weight):
    span = SPAN
    rows, chans = signal.shape
    blocks = block_perm.shape[0]
    seq = blocks * span
    n_ctx = seq // rows
    per_dev = chans // n_ctx
    ctx_index = lax.axis_index("ctx")

    def to_channel_major(a):
        return lax.all_to_all(a, "ctx", 1, 0, tiled=True).T

    inverse = (
        jnp.zeros((blocks,), jnp.int32).at[block_perm].set(jnp.arange(blocks, dtype=jnp.int32))
    )

    def slots_to_natural(a):
        return jnp.take(a.reshape(per_dev, blocks, span), inverse, axis=1).reshape(per_dev, seq)

    x_cm = slots_to_natural(to_channel_major(signal))
    g_cm = slots_to_natural(to_channel_major(gate))
    f_cm = to_channel_major(filt)
    bias_cm = lax.dynamic_slice_in_dim(bias, ctx_index * per_dev, per_dev)
    group = 4
    conv = lax.map(
        lambda xf: block_conv(xf[0], xf[1], doc_ids),
        (x_cm.reshape(per_dev // group, group, seq), f_cm.reshape(per_dev // group, group, seq)),
    ).reshape(per_dev, seq)
    gated = (
        g_cm.astype(jnp.float32) * (conv + bias_cm[:, None] * x_cm.astype(jnp.float32))
    ).astype(jnp.bfloat16)
    gated_slots = jnp.take(gated.reshape(per_dev, blocks, span), block_perm, axis=1)
    gated_slots = gated_slots.reshape(per_dev, seq).T
    gated_local = lax.all_to_all(gated_slots, "ctx", 0, 1, tiled=True)
    partial_value = jnp.dot(gated_local, out_weight, preferred_element_type=jnp.float32)
    return lax.psum_scatter(partial_value, "tp", scatter_dimension=1, tiled=True).astype(
        jnp.bfloat16
    )


def solution(mesh):
    return jax.shard_map(
        body,
        mesh=mesh,
        in_specs=(P("ctx", "tp"), P("ctx", "tp"), P("ctx", "tp"), P("tp"), P(), P(), P("tp", None)),
        out_specs=P("ctx", "tp"),
        check_vma=False,
    )
```

profile of v0, /device:TPU:1, one launch (start us, length us, event | category | flops | bytes accessed | tf_op | source)
XLA Modules:
  0.0 430.1 jit_solution(5247840323906330248)
XLA Ops:
  8.3 9.7 %all-to-all-start.1 = ((bf16[128,32,16]{0,2,1:T(8,128)(2,1)}), bf16[128,32,16]{0,2,1:T(8,128)(2,1)S(1)}, u32[]{:S(2)}, u32[]{:S(2)}) async-start(bf16[128,32,16]{0,2,1:T(8,128)(2,1)} %bitcast.15), calls=%async_computation.1 | async-start | bytes 262144 | tf_op jit(solution)/shard_map/all_to_all | solution.py:63
  25.7 6.9 %all-to-all-start.2 = ((bf16[128,32,16]{0,2,1:T(8,128)(2,1)}), bf16[128,32,16]{0,2,1:T(8,128)(2,1)S(1)}, u32[]{:S(2)}, u32[]{:S(2)}) async-start(bf16[128,32,16]{0,2,1:T(8,128)(2,1)} %bitcast.19), calls=%async_computation.2 | async-start | bytes 262144 | tf_op jit(solution)/shard_map/all_to_all | solution.py:63
  44.2 323.2 %while.12 = (s32[]{:T(128)}, f32[4,4,4096]{2,1,0:T(4,128)}, s32[4096]{0:T(1024)S(1)}, bf16[4,4,4096]{2,1,0:T(4,128)(2,1)S(1)}, bf16[4,4,4096]{2,1,0:T(4,128)(2,1)S(1)}, /*index=5*/s32[]{:T(128)}, bf16[]{:T(256)}) while((s32[]{:T(128)}, f32[4,4,4096]{2,1,0:T(4,128)}, s32[4096]{0:T(1024)S(1)}, bf16[4,4,4096]{2,1,0:T(4,128)(2,1)S(1)}, ...), condition=%wide.region_2.4_spmd, body=%wide.region_1.0_spmd.sunk | while | flops 144167168 | bytes 68822360 | solution.py:77
  59.2 6.4 %reshape.234 = bf16[4,64,4159]{2,1,0:T(8,128)(2,1)} reshape(bf16[1064704]{0:T(1024)(128)(2,1)} %reshape.233) | data formatting | bytes 4258816 | tf_op jit(solution)/shard_map/while/body/eval_jaxpr/reshape | solution.py:25
  68.8 6.9 %reshape.235 = bf16[4,64,64,64]{3,2,1,0:T(8,128)(2,1)} reshape(bf16[4,64,4096]{2,1,0:T(8,128)(2,1)} %slice.80) | data formatting | bytes 4194304 | tf_op jit(solution)/shard_map/while/body/eval_jaxpr/reshape | solution.py:26
  80.0 7.3 %reshape.238 = bf16[4,8192,64]{1,2,0:T(8,128)(2,1)} reshape(bf16[4,64,128,64]{2,1,3,0:T(8,128)(2,1)} %broadcast_in_dim.226) | data formatting | bytes 8388608 | tf_op jit(solution)/shard_map/while/body/eval_jaxpr/reshape | solution.py:14
  87.4 19.3 %reshape.239 = bf16[4,64,127,64]{2,1,3,0:T(8,128)(2,1)} reshape(bf16[4,8128,64]{1,2,0:T(8,128)(2,1)} %bitcast.133) | data formatting | bytes 8323072 | tf_op jit(solution)/shard_map/while/body/eval_jaxpr/reshape | solution.py:15
  111.1 6.4 %reshape.241 = s32[1,64,127,64]{2,1,3,0:T(8,128)} reshape(s32[1,8128,64]{1,2,0:T(8,128)} %bitcast.135) | data formatting | bytes 4161536 | tf_op jit(solution)/shard_map/while/body/eval_jaxpr/reshape | solution.py:15
  140.0 6.4 %reshape.234 = bf16[4,64,4159]{2,1,0:T(8,128)(2,1)} reshape(bf16[1064704]{0:T(1024)(128)(2,1)} %reshape.233) | data formatting | bytes 4258816 | tf_op jit(solution)/shard_map/while/body/eval_jaxpr/reshape | solution.py:25
  149.5 6.9 %reshape.235 = bf16[4,64,64,64]{3,2,1,0:T(8,128)(2,1)} reshape(bf16[4,64,4096]{2,1,0:T(8,128)(2,1)} %slice.80) | data formatting | bytes 4194304 | tf_op jit(solution)/shard_map/while/body/eval_jaxpr/reshape | solution.py:26
  160.8 7.3 %reshape.238 = bf16[4,8192,64]{1,2,0:T(8,128)(2,1)} reshape(bf16[4,64,128,64]{2,1,3,0:T(8,128)(2,1)} %broadcast_in_dim.226) | data formatting | bytes 8388608 | tf_op jit(solution)/shard_map/while/body/eval_jaxpr/reshape | solution.py:14
  168.1 19.3 %reshape.239 = bf16[4,64,127,64]{2,1,3,0:T(8,128)(2,1)} reshape(bf16[4,8128,64]{1,2,0:T(8,128)(2,1)} %bitcast.133) | data formatting | bytes 8323072 | tf_op jit(solution)/shard_map/while/body/eval_jaxpr/reshape | solution.py:15
  191.8 6.4 %reshape.241 = s32[1,64,127,64]{2,1,3,0:T(8,128)} reshape(s32[1,8128,64]{1,2,0:T(8,128)} %bitcast.135) | data formatting | bytes 4161536 | tf_op jit(solution)/shard_map/while/body/eval_jaxpr/reshape | solution.py:15
  220.7 6.4 %reshape.234 = bf16[4,64,4159]{2,1,0:T(8,128)(2,1)} reshape(bf16[1064704]{0:T(1024)(128)(2,1)} %reshape.233) | data formatting | bytes 4258816 | tf_op jit(solution)/shard_map/while/body/eval_jaxpr/reshape | solution.py:25
  230.3 6.9 %reshape.235 = bf16[4,64,64,64]{3,2,1,0:T(8,128)(2,1)} reshape(bf16[4,64,4096]{2,1,0:T(8,128)(2,1)} %slice.80) | data formatting | bytes 4194304 | tf_op jit(solution)/shard_map/while/body/eval_jaxpr/reshape | solution.py:26
  241.6 7.3 %reshape.238 = bf16[4,8192,64]{1,2,0:T(8,128)(2,1)} reshape(bf16[4,64,128,64]{2,1,3,0:T(8,128)(2,1)} %broadcast_in_dim.226) | data formatting | bytes 8388608 | tf_op jit(solution)/shard_map/while/body/eval_jaxpr/reshape | solution.py:14
  248.9 19.3 %reshape.239 = bf16[4,64,127,64]{2,1,3,0:T(8,128)(2,1)} reshape(bf16[4,8128,64]{1,2,0:T(8,128)(2,1)} %bitcast.133) | data formatting | bytes 8323072 | tf_op jit(solution)/shard_map/while/body/eval_jaxpr/reshape | solution.py:15
  301.5 6.4 %reshape.234 = bf16[4,64,4159]{2,1,0:T(8,128)(2,1)} reshape(bf16[1064704]{0:T(1024)(128)(2,1)} %reshape.233) | data formatting | bytes 4258816 | tf_op jit(solution)/shard_map/while/body/eval_jaxpr/reshape | solution.py:25
  311.0 6.9 %reshape.235 = bf16[4,64,64,64]{3,2,1,0:T(8,128)(2,1)} reshape(bf16[4,64,4096]{2,1,0:T(8,128)(2,1)} %slice.80) | data formatting | bytes 4194304 | tf_op jit(solution)/shard_map/while/body/eval_jaxpr/reshape | solution.py:26
  322.3 7.3 %reshape.238 = bf16[4,8192,64]{1,2,0:T(8,128)(2,1)} reshape(bf16[4,64,128,64]{2,1,3,0:T(8,128)(2,1)} %broadcast_in_dim.226) | data formatting | bytes 8388608 | tf_op jit(solution)/shard_map/while/body/eval_jaxpr/reshape | solution.py:14
  329.7 19.3 %reshape.239 = bf16[4,64,127,64]{2,1,3,0:T(8,128)(2,1)} reshape(bf16[4,8128,64]{1,2,0:T(8,128)(2,1)} %bitcast.133) | data formatting | bytes 8323072 | tf_op jit(solution)/shard_map/while/body/eval_jaxpr/reshape | solution.py:15
  353.4 6.4 %reshape.241 = s32[1,64,127,64]{2,1,3,0:T(8,128)} reshape(s32[1,8128,64]{1,2,0:T(8,128)} %bitcast.135) | data formatting | bytes 4161536 | tf_op jit(solution)/shard_map/while/body/eval_jaxpr/reshape | solution.py:15
  372.1 15.1 %all_to_all.76 = bf16[32,128,16]{1,2,0:T(8,128)(2,1)S(1)} all-to-all(bf16[32,128,16]{1,2,0:T(8,128)(2,1)S(1)} %copy_bitcast_fusion.1), channel_id=1, replica_groups=mesh['ctx'=32,'tp'=4] {'ctx'}, dimensions={0} | all-to-all | bytes 262144 | tf_op jit(solution)/shard_map/all_to_all | solution.py:86
  388.6 33.0 %reduce-scatter.2.cloned.1.call-done = f32[128,512]{1,0:T(8,128)} async-done(((f32[128,2048]{1,0:T(8,128)}), f32[128,512]{1,0:T(8,128)}) %reduce-scatter.2.cloned.1.call-update) | async-done | bytes 262160 | tf_op jit(solution)/shard_map/reduce_scatter | solution.py:88
  (170 shorter events, 172.3 us)
Async XLA Ops:
  6.5 380.6 %copy-start = (bf16[512,2048]{1,0:T(8,128)(2,1)S(1)}, bf16[512,2048]{1,0:T(8,128)(2,1)}, u32[]{:S(2)}) copy-start(bf16[512,2048]{1,0:T(8,128)(2,1)} %param.17) | copy-start | bytes 6291460
  8.3 17.3 %all-to-all-start.1 = ((bf16[128,32,16]{0,2,1:T(8,128)(2,1)}), bf16[128,32,16]{0,2,1:T(8,128)(2,1)S(1)}, u32[]{:S(2)}, u32[]{:S(2)}) async-start(bf16[128,32,16]{0,2,1:T(8,128)(2,1)} %bitcast.15), calls=%async_computation.1 | async-start | bytes 262144 | tf_op jit(solution)/shard_map/all_to_all | solution.py:63
  23.6 20.7 %copy-start.1 = (s32[4096]{0:T(1024)S(1)}, s32[4096]{0:T(1024)}, u32[]{:S(2)}) copy-start(s32[4096]{0:T(1024)} %param.15) | copy-start | bytes 49156
  25.7 14.5 %all-to-all-start.2 = ((bf16[128,32,16]{0,2,1:T(8,128)(2,1)}), bf16[128,32,16]{0,2,1:T(8,128)(2,1)S(1)}, u32[]{:S(2)}, u32[]{:S(2)}) async-start(bf16[128,32,16]{0,2,1:T(8,128)(2,1)} %bitcast.19), calls=%async_computation.2 | async-start | bytes 262144 | tf_op jit(solution)/shard_map/all_to_all | solution.py:63
  40.2 328.5 %all-to-all-start = ((bf16[128,32,16]{0,2,1:T(8,128)(2,1)}), bf16[128,32,16]{0,2,1:T(8,128)(2,1)S(1)}, u32[]{:S(2)}, u32[]{:S(2)}) async-start(bf16[128,32,16]{0,2,1:T(8,128)(2,1)} %bitcast.11), calls=%async_computation | async-start | bytes 262144 | tf_op jit(solution)/shard_map/all_to_all | solution.py:63
  44.1 377.6 %reduce-scatter.2.cloned.1.call-start = ((), (), s32[]{:S(2)}) async-start(), calls=%async_computation.5 | async-start | bytes 1310720 | tf_op jit(solution)/shard_map/reduce_scatter | solution.py:88
Sparse Core Ops, SparseCore 0:
  388.7 32.8 reduce-scatter.1
where the time goes:
time: 433 us; the launch traced here: 430 us
  local copies, waits for them, and re-layouts  305 us (70%)
  waiting for transfers between devices  39.9 us (9%)
  matrix products  23.5 us (5%)
  starting transfers between devices  20.6 us (5%)
  blocking collectives  15.1 us (3%)
  between operations  13.6 us (3%)
  other arithmetic  12.4 us (3%)
    reshape x8, local copies, waits for them, and re-layouts, skew_blocks(): return tiled.reshape(chans, blocks, 2 * blocks - 1, span)[:, :, :blocks]  103 us
    while x16, local copies, waits for them, and re-layouts  37.3 us
    reduce_scatter x1, waiting for transfers between devices, body(): lax.psum_scatter(partial_value, 'tp', scatter_dimension=1, tiled=True)  33 us
    reshape x4, local copies, waits for them, and re-layouts, skew_blocks(): tiled.reshape(chans, blocks * 2 * blocks, span)  29.3 us
    reshape x4, local copies, waits for them, and re-layouts, block_conv(): tt = tt.reshape(chans, span, blocks, span)  27.6 us
    broadcast_in_dim x20, local copies, waits for them, and re-layouts, skew_blocks(): tiled = jnp.broadcast_to(a_ext[:, None], (chans, blocks, 2 * blocks, span))  27.4 us
    reshape x4, local copies, waits for them, and re-layouts, block_conv(): tt = tt[:, :span * (width - 1)].reshape(chans, span, width - 1)[:, :, :seq]  25.7 us
    all_to_all x3, starting transfers between devices, to_channel_major(): return lax.all_to_all(a, 'ctx', 1, 0, tiled=True).T  20.5 us
  transfers between devices with their start and end apart: 4, of which 3 were waited for; matrix products, arithmetic and copies ran while one was open for 77% of the time, Pallas kernels for 0%

commit v1 on v0

--- a/solution.py
+++ b/solution.py
@@ -5,6 +5,15 @@
 
 SPAN = 64
 DOC_COUNT = 4
+
+
+def matrix_turn(w_in):
+    x_new = jax.lax.axis_size("ctx")
+    earlier = jnp.split(w_in, x_new, axis=0)
+    w2 = jnp.stack(earlier)
+    step_out = jax.lax.all_to_all(w2, axis_name="ctx", split_axis=0, concat_axis=0)
+    front = jnp.concatenate(step_out, 1)
+    return front
 
 
 def skew_blocks(a, fill):
@@ -83,7 +92,7 @@
     ).astype(jnp.bfloat16)
     gated_slots = jnp.take(gated.reshape(per_dev, blocks, span), block_perm, axis=1)
     gated_slots = gated_slots.reshape(per_dev, seq).T
-    gated_local = lax.all_to_all(gated_slots, "ctx", 0, 1, tiled=True)
+    gated_local = matrix_turn(gated_slots)
     partial_value = jnp.dot(gated_local, out_weight, preferred_element_type=jnp.float32)
     return lax.psum_scatter(partial_value, "tp", scatter_dimension=1, tiled=True).astype(
         jnp.bfloat16

time: 433 us -> 433 us (level)
  no operation moved by 1% of the time
where the time goes in v1:
time: 433 us; the launch traced here: 430 us
  local copies, waits for them, and re-layouts  305 us (70%)
  waiting for transfers between devices  39.9 us (9%)
  matrix products  23.5 us (5%)
  starting transfers between devices  20.5 us (5%)
  blocking collectives  15.1 us (3%)
  between operations  13.6 us (3%)
  other arithmetic  12.4 us (3%)
    reshape x8, local copies, waits for them, and re-layouts, skew_blocks(): return tiled.reshape(chans, blocks, 2 * blocks - 1, span)[:, :, :blocks]  103 us
    while x16, local copies, waits for them, and re-layouts  37.2 us
    reduce_scatter x1, waiting for transfers between devices, body(): lax.psum_scatter(partial_value, 'tp', scatter_dimension=1, tiled=True)  33 us
    reshape x4, local copies, waits for them, and re-layouts, skew_blocks(): tiled.reshape(chans, blocks * 2 * blocks, span)  29.3 us
    reshape x4, local copies, waits for them, and re-layouts, block_conv(): tt = tt.reshape(chans, span, blocks, span)  27.5 us
    broadcast_in_dim x20, local copies, waits for them, and re-layouts, skew_blocks(): tiled = jnp.broadcast_to(a_ext[:, None], (chans, blocks, 2 * blocks, span))  27.4 us
    reshape x4, local copies, waits for them, and re-layouts, block_conv(): tt = tt[:, :span * (width - 1)].reshape(chans, span, width - 1)[:, :, :seq]  25.7 us
    all_to_all x3, starting transfers between devices, to_channel_major(): return lax.all_to_all(a, 'ctx', 1, 0, tiled=True).T  20.5 us
  transfers between devices with their start and end apart: 4, of which 3 were waited for; matrix products, arithmetic and copies ran while one was open for 77% of the time, Pallas kernels for 0%

profile of v1, /device:TPU:1, one launch (start us, length us, event | category | flops | bytes accessed | tf_op | source)
XLA Modules:
  0.0 430.1 jit_solution(5212129369680612735)
XLA Ops:
  8.3 9.7 %all-to-all-start.1 = ((bf16[128,32,16]{0,2,1:T(8,128)(2,1)}), bf16[128,32,16]{0,2,1:T(8,128)(2,1)S(1)}, u32[]{:S(2)}, u32[]{:S(2)}) async-start(bf16[128,32,16]{0,2,1:T(8,128)(2,1)} %bitcast.15), calls=%async_computation.1 | async-start | bytes 262144 | tf_op jit(solution)/shard_map/all_to_all | solution.py:72
  25.7 6.9 %all-to-all-start.2 = ((bf16[128,32,16]{0,2,1:T(8,128)(2,1)}), bf16[128,32,16]{0,2,1:T(8,128)(2,1)S(1)}, u32[]{:S(2)}, u32[]{:S(2)}) async-start(bf16[128,32,16]{0,2,1:T(8,128)(2,1)} %bitcast.19), calls=%async_computation.2 | async-start | bytes 262144 | tf_op jit(solution)/shard_map/all_to_all | solution.py:72
  44.2 323.0 %while.12 = (s32[]{:T(128)}, f32[4,4,4096]{2,1,0:T(4,128)}, s32[4096]{0:T(1024)S(1)}, bf16[4,4,4096]{2,1,0:T(4,128)(2,1)S(1)}, bf16[4,4,4096]{2,1,0:T(4,128)(2,1)S(1)}, /*index=5*/s32[]{:T(128)}, bf16[]{:T(256)}) while((s32[]{:T(128)}, f32[4,4,4096]{2,1,0:T(4,128)}, s32[4096]{0:T(1024)S(1)}, bf16[4,4,4096]{2,1,0:T(4,128)(2,1)S(1)}, ...), condition=%wide.region_2.4_spmd, body=%wide.region_1.0_spmd.sunk | while | flops 144167168 | bytes 68822360 | solution.py:86
  59.1 6.4 %reshape.239 = bf16[4,64,4159]{2,1,0:T(8,128)(2,1)} reshape(bf16[1064704]{0:T(1024)(128)(2,1)} %reshape.238) | data formatting | bytes 4258816 | tf_op jit(solution)/shard_map/while/body/eval_jaxpr/reshape | solution.py:34
  68.7 6.9 %reshape.240 = bf16[4,64,64,64]{3,2,1,0:T(8,128)(2,1)} reshape(bf16[4,64,4096]{2,1,0:T(8,128)(2,1)} %slice.80) | data formatting | bytes 4194304 | tf_op jit(solution)/shard_map/while/body/eval_jaxpr/reshape | solution.py:35
  80.0 7.3 %reshape.243 = bf16[4,8192,64]{1,2,0:T(8,128)(2,1)} reshape(bf16[4,64,128,64]{2,1,3,0:T(8,128)(2,1)} %broadcast_in_dim.226) | data formatting | bytes 8388608 | tf_op jit(solution)/shard_map/while/body/eval_jaxpr/reshape | solution.py:23
  87.3 19.3 %reshape.244 = bf16[4,64,127,64]{2,1,3,0:T(8,128)(2,1)} reshape(bf16[4,8128,64]{1,2,0:T(8,128)(2,1)} %bitcast.256) | data formatting | bytes 8323072 | tf_op jit(solution)/shard_map/while/body/eval_jaxpr/reshape | solution.py:24
  111.0 6.4 %reshape.246 = s32[1,64,127,64]{2,1,3,0:T(8,128)} reshape(s32[1,8128,64]{1,2,0:T(8,128)} %bitcast.258) | data formatting | bytes 4161536 | tf_op jit(solution)/shard_map/while/body/eval_jaxpr/reshape | solution.py:24
  139.8 6.4 %reshape.239 = bf16[4,64,4159]{2,1,0:T(8,128)(2,1)} reshape(bf16[1064704]{0:T(1024)(128)(2,1)} %reshape.238) | data formatting | bytes 4258816 | tf_op jit(solution)/shard_map/while/body/eval_jaxpr/reshape | solution.py:34
  149.4 6.9 %reshape.240 = bf16[4,64,64,64]{3,2,1,0:T(8,128)(2,1)} reshape(bf16[4,64,4096]{2,1,0:T(8,128)(2,1)} %slice.80) | data formatting | bytes 4194304 | tf_op jit(solution)/shard_map/while/body/eval_jaxpr/reshape | solution.py:35
  160.7 7.3 %reshape.243 = bf16[4,8192,64]{1,2,0:T(8,128)(2,1)} reshape(bf16[4,64,128,64]{2,1,3,0:T(8,128)(2,1)} %broadcast_in_dim.226) | data formatting | bytes 8388608 | tf_op jit(solution)/shard_map/while/body/eval_jaxpr/reshape | solution.py:23
  168.0 19.3 %reshape.244 = bf16[4,64,127,64]{2,1,3,0:T(8,128)(2,1)} reshape(bf16[4,8128,64]{1,2,0:T(8,128)(2,1)} %bitcast.256) | data formatting | bytes 8323072 | tf_op jit(solution)/shard_map/while/body/eval_jaxpr/reshape | solution.py:24
  191.7 6.4 %reshape.246 = s32[1,64,127,64]{2,1,3,0:T(8,128)} reshape(s32[1,8128,64]{1,2,0:T(8,128)} %bitcast.258) | data formatting | bytes 4161536 | tf_op jit(solution)/shard_map/while/body/eval_jaxpr/reshape | solution.py:24
  220.5 6.4 %reshape.239 = bf16[4,64,4159]{2,1,0:T(8,128)(2,1)} reshape(bf16[1064704]{0:T(1024)(128)(2,1)} %reshape.238) | data formatting | bytes 4258816 | tf_op jit(solution)/shard_map/while/body/eval_jaxpr/reshape | solution.py:34
  230.1 6.9 %reshape.240 = bf16[4,64,64,64]{3,2,1,0:T(8,128)(2,1)} reshape(bf16[4,64,4096]{2,1,0:T(8,128)(2,1)} %slice.80) | data formatting | bytes 4194304 | tf_op jit(solution)/shard_map/while/body/eval_jaxpr/reshape | solution.py:35
  241.3 7.3 %reshape.243 = bf16[4,8192,64]{1,2,0:T(8,128)(2,1)} reshape(bf16[4,64,128,64]{2,1,3,0:T(8,128)(2,1)} %broadcast_in_dim.226) | data formatting | bytes 8388608 | tf_op jit(solution)/shard_map/while/body/eval_jaxpr/reshape | solution.py:23
  248.7 19.3 %reshape.244 = bf16[4,64,127,64]{2,1,3,0:T(8,128)(2,1)} reshape(bf16[4,8128,64]{1,2,0:T(8,128)(2,1)} %bitcast.256) | data formatting | bytes 8323072 | tf_op jit(solution)/shard_map/while/body/eval_jaxpr/reshape | solution.py:24
  272.3 6.4 %reshape.246 = s32[1,64,127,64]{2,1,3,0:T(8,128)} reshape(s32[1,8128,64]{1,2,0:T(8,128)} %bitcast.258) | data formatting | bytes 4161536 | tf_op jit(solution)/shard_map/while/body/eval_jaxpr/reshape | solution.py:24
  301.2 6.4 %reshape.239 = bf16[4,64,4159]{2,1,0:T(8,128)(2,1)} reshape(bf16[1064704]{0:T(1024)(128)(2,1)} %reshape.238) | data formatting | bytes 4258816 | tf_op jit(solution)/shard_map/while/body/eval_jaxpr/reshape | solution.py:34
  310.7 6.9 %reshape.240 = bf16[4,64,64,64]{3,2,1,0:T(8,128)(2,1)} reshape(bf16[4,64,4096]{2,1,0:T(8,128)(2,1)} %slice.80) | data formatting | bytes 4194304 | tf_op jit(solution)/shard_map/while/body/eval_jaxpr/reshape | solution.py:35
  322.0 7.3 %reshape.243 = bf16[4,8192,64]{1,2,0:T(8,128)(2,1)} reshape(bf16[4,64,128,64]{2,1,3,0:T(8,128)(2,1)} %broadcast_in_dim.226) | data formatting | bytes 8388608 | tf_op jit(solution)/shard_map/while/body/eval_jaxpr/reshape | solution.py:23
  329.4 19.3 %reshape.244 = bf16[4,64,127,64]{2,1,3,0:T(8,128)(2,1)} reshape(bf16[4,8128,64]{1,2,0:T(8,128)(2,1)} %bitcast.256) | data formatting | bytes 8323072 | tf_op jit(solution)/shard_map/while/body/eval_jaxpr/reshape | solution.py:24
  372.1 15.1 %all_to_all.62 = bf16[32,128,16]{1,2,0:T(8,128)(2,1)S(1)} all-to-all(bf16[32,128,16]{1,2,0:T(8,128)(2,1)S(1)} %constant_dynamic-update-slice_fusion.1), channel_id=1, replica_groups=mesh['ctx'=32,'tp'=4] {'ctx'}, dimensions={0} | all-to-all | bytes 262144 | tf_op jit(solution)/shard_map/all_to_all | solution.py:14
  388.6 33.0 %reduce-scatter.2.cloned.1.call-done = f32[128,512]{1,0:T(8,128)} async-done(((f32[128,2048]{1,0:T(8,128)}), f32[128,512]{1,0:T(8,128)}) %reduce-scatter.2.cloned.1.call-update) | async-done | bytes 262160 | tf_op jit(solution)/shard_map/reduce_scatter | solution.py:97
  (200 shorter events, 172.4 us)
Async XLA Ops:
  6.5 380.6 %copy-start = (bf16[512,2048]{1,0:T(8,128)(2,1)S(1)}, bf16[512,2048]{1,0:T(8,128)(2,1)}, u32[]{:S(2)}) copy-start(bf16[512,2048]{1,0:T(8,128)(2,1)} %param.17) | copy-start | bytes 6291460
  8.3 17.3 %all-to-all-start.1 = ((bf16[128,32,16]{0,2,1:T(8,128)(2,1)}), bf16[128,32,16]{0,2,1:T(8,128)(2,1)S(1)}, u32[]{:S(2)}, u32[]{:S(2)}) async-start(bf16[128,32,16]{0,2,1:T(8,128)(2,1)} %bitcast.15), calls=%async_computation.1 | async-start | bytes 262144 | tf_op jit(solution)/shard_map/all_to_all | solution.py:72
  23.5 20.6 %copy-start.1 = (s32[4096]{0:T(1024)S(1)}, s32[4096]{0:T(1024)}, u32[]{:S(2)}) copy-start(s32[4096]{0:T(1024)} %param.15) | copy-start | bytes 49156
  25.7 14.5 %all-to-all-start.2 = ((bf16[128,32,16]{0,2,1:T(8,128)(2,1)}), bf16[128,32,16]{0,2,1:T(8,128)(2,1)S(1)}, u32[]{:S(2)}, u32[]{:S(2)}) async-start(bf16[128,32,16]{0,2,1:T(8,128)(2,1)} %bitcast.19), calls=%async_computation.2 | async-start | bytes 262144 | tf_op jit(solution)/shard_map/all_to_all | solution.py:72
  40.2 328.2 %all-to-all-start = ((bf16[128,32,16]{0,2,1:T(8,128)(2,1)}), bf16[128,32,16]{0,2,1:T(8,128)(2,1)S(1)}, u32[]{:S(2)}, u32[]{:S(2)}) async-start(bf16[128,32,16]{0,2,1:T(8,128)(2,1)} %bitcast.11), calls=%async_computation | async-start | bytes 262144 | tf_op jit(solution)/shard_map/all_to_all | solution.py:72
  44.0 377.6 %reduce-scatter.2.cloned.1.call-start = ((), (), s32[]{:S(2)}) async-start(), calls=%async_computation.5 | async-start | bytes 1310720 | tf_op jit(solution)/shard_map/reduce_scatter | solution.py:97
Sparse Core Ops, SparseCore 0:
  388.8 32.8 reduce-scatter.1
